TPU v7x, 512 devices: a whole 4x8x8 slice. The times are simulated.
512 devices in a mesh: ctx: 32 (over z, y_lo), head: 16 (over y_hi, x, core).
Axes of the slice: x: 4, y: 8 (y_hi: 2, y_lo: 4; y = y_hi * 4 + y_lo), z: 8, core: 2. Of those that a mesh axis runs over, the one named last changes fastest.
Arguments:
- queries: bfloat16 [12288, 4096], P('ctx', 'head'), may hold values from -6 to 6
- keys: bfloat16 [12288, 4096], P('ctx', 'head'), may hold values from -6 to 6
- values: bfloat16 [12288, 4096], P('ctx', 'head'), may hold values from -6 to 6
- out_weight: bfloat16 [4096, 5120], P('head'), may hold values from -1.1953125 to 1.1953125
- neighbours: int32 [32, 7], P('ctx'), may hold values from -1 to 31, as said below
- counts: int32 [32], P('ctx'), may hold values from 1 to 7
Outputs:
- projected: bfloat16 [12288, 5120], P(('ctx', 'head'))
Inputs may be any that keep to these rules, and one draw needn't show every extreme that they name: `neighbours`: for query tile g the first counts[g] entries are distinct tiles within 3 of g, g itself among them; the other entries are -1. Some tile lists 7 tiles.
All inputs are finite; a program needn't handle non-finite values.
Results may differ from a plain program's by a relative error of at most 0.019.
Values may be sent and summed in bfloat16 or wider, within the bound.
A program may use at most 64 MiB of HBM per device.

v0:
```python
import math

import jax
import jax.numpy as jnp
from jax import lax
from jax.sharding import PartitionSpec as P

HD = 128
REACH = 3


def passed_along(value, axis, steps):
    count = lax.axis_size(axis)
    first, last = (max(0, -steps), min(count, count - steps))
    return lax.ppermute(value, axis, [(source, source + steps) for source in range(first, last)])


def local(queries, keys, values, out_weight, neighbours, counts):
    row_count, feat_width = queries.shape
    tiles_dev = counts.shape[0]
    tile_rows = row_count // tiles_dev
    reach_dev = (REACH + tiles_dev - 1) // tiles_dev
    window_tiles = 2 * REACH + 1
    ctx_total = lax.axis_size("ctx")
    ctx_index = lax.axis_index("ctx")
    lower_keys = []
    lower_values = []
    upper_keys = []
    upper_values = []
    for distance in range(1, reach_dev + 1):
        from_below = passed_along((keys, values), "ctx", distance)
        from_above = passed_along((keys, values), "ctx", -distance)
        lower_keys.insert(0, from_below[0])
        lower_values.insert(0, from_below[1])
        upper_keys.append(from_above[0])
        upper_values.append(from_above[1])
    key_window = jnp.concatenate(lower_keys + [keys] + upper_keys, axis=0)
    value_window = jnp.concatenate(lower_values + [values] + upper_values, axis=0)
    heads_dev = feat_width // HD
    tile_total = tiles_dev * ctx_total
    offsets = jnp.arange(window_tiles, dtype=jnp.int32) - REACH
    slot_index = jnp.arange(window_tiles, dtype=jnp.int32)
    scale = 1.0 / math.sqrt(HD)

    def one_tile(local_tile):
        tile_index = ctx_index * tiles_dev + local_tile
        target = tile_index + offsets
        listing = lax.dynamic_index_in_dim(neighbours, local_tile, 0, keepdims=False)
        slot_count = lax.dynamic_index_in_dim(counts, local_tile, 0, keepdims=False)
        member = jnp.any(
            (listing[None, :] == target[:, None]) & (slot_index[None, :] < slot_count), axis=1
        )
        allowed = member & (target >= 0) & (target < tile_total)
        key_mask = jnp.repeat(allowed, tile_rows)

        def one_head(head_index):
            q_head = lax.dynamic_slice_in_dim(queries, head_index * HD, HD, 1)
            k_head = lax.dynamic_slice_in_dim(key_window, head_index * HD, HD, 1)
            v_head = lax.dynamic_slice_in_dim(value_window, head_index * HD, HD, 1)
            scores = (
                jnp.einsum("qd,kd->qk", q_head, k_head, preferred_element_type=jnp.float32) * scale
            )
            scores = jnp.where(key_mask[None, :], scores, -1e30)
            row_max = jnp.max(scores, axis=1, keepdims=True)
            weights = jnp.where(key_mask[None, :], jnp.exp(scores - row_max), 0.0)
            weight_sum = jnp.sum(weights, axis=1, keepdims=True)
            weights_low = weights.astype(jnp.bfloat16)
            mixed = jnp.dot(weights_low, v_head, preferred_element_type=jnp.float32) / weight_sum
            return mixed.astype(jnp.bfloat16)

        per_head = lax.map(one_head, jnp.arange(heads_dev, dtype=jnp.int32))
        return jnp.transpose(per_head, (1, 0, 2)).reshape(tile_rows, feat_width)

    attended = lax.map(one_tile, jnp.arange(tiles_dev, dtype=jnp.int32)).reshape(
        row_count, feat_width
    )
    return lax.psum_scatter(
        jnp.dot(attended, out_weight, preferred_element_type=jnp.float32).astype(jnp.bfloat16),
        "head",
        scatter_dimension=0,
        tiled=True,
    )


def solution(mesh):
    placed = (
        P("ctx", "head"),
        P("ctx", "head"),
        P("ctx", "head"),
        P("head", None),
        P("ctx", None),
        P("ctx"),
    )
    return jax.shard_map(
        local, mesh=mesh, in_specs=placed, out_specs=P(("ctx", "head"), None), check_vma=False
    )
```

profile of v0, /device:TPU:8, one launch (start us, length us, event | category | flops | bytes accessed | tf_op | source)
XLA Modules:
  0.0 219.7 jit_solution(819193738379309867)
XLA Ops:
  6.5 0.0 copy-start
  6.5 0.0 copy-start.3
  6.5 0.0 reduce-scatter.2.cloned.1.call-start
  6.5 5.1 %collective-permute-start = (bf16[384,256]{1,0:T(8,128)(2,1)}, bf16[384,256]{1,0:T(8,128)(2,1)}, u32[]{:S(2)}, u32[]{:S(2)}) collective-permute-start(bf16[384,256]{1,0:T(8,128)(2,1)} %param.9), channel_id=1, source_target_pairs={{0,48},{16,64},{32,80},{48,96},{64,112},{80,128},{96,144},{112,160... | collective-permute-start | bytes 589832 | tf_op jit(solution)/shard_map/ppermute | solution.py:15
  11.6 4.5 %collective-permute-start.1 = (bf16[384,256]{1,0:T(8,128)(2,1)}, bf16[384,256]{1,0:T(8,128)(2,1)}, u32[]{:S(2)}, u32[]{:S(2)}) collective-permute-start(bf16[384,256]{1,0:T(8,128)(2,1)} %param.9), channel_id=1, source_target_pairs={{0,32},{16,48},{32,64},{48,80},{64,96},{80,112},{96,128},{112,144}... | collective-permute-start | bytes 589832 | tf_op jit(solution)/shard_map/ppermute | solution.py:15
  16.1 3.7 %collective-permute-start.2 = (bf16[384,256]{1,0:T(8,128)(2,1)}, bf16[384,256]{1,0:T(8,128)(2,1)S(1)}, u32[]{:S(2)}, u32[]{:S(2)}) collective-permute-start(bf16[384,256]{1,0:T(8,128)(2,1)} %param.9), channel_id=1, source_target_pairs={{0,16},{16,32},{32,48},{48,64},{64,80},{80,96},{96,112},{112,128},... | collective-permute-start | bytes 589832 | tf_op jit(solution)/shard_map/ppermute | solution.py:15
  19.9 2.1 collective-permute-start.3
  22.0 1.3 collective-permute-start.4
  24.0 0.8 and_reduce_fusion
  24.8 0.0 collective-permute-done
  24.8 1.3 collective-permute-start.5
  26.1 0.9 constant_dynamic-update-slice_fusion.7
  27.1 0.0 collective-permute-done.1
  27.1 9.6 %collective-permute-start.6 = (bf16[384,256]{1,0:T(8,128)(2,1)}, bf16[384,256]{1,0:T(8,128)(2,1)S(1)}, u32[]{:S(2)}, u32[]{:S(2)}) collective-permute-start(bf16[384,256]{1,0:T(8,128)(2,1)} %param.10), channel_id=1, source_target_pairs={{0,48},{16,64},{32,80},{48,96},{64,112},{80,128},{96,144},{112,160... | collective-permute-start | bytes 589832 | tf_op jit(solution)/shard_map/ppermute | solution.py:15
  36.7 0.9 constant_dynamic-update-slice_fusion.6
  37.7 0.0 collective-permute-done.2
  37.7 2.7 %collective-permute-start.7 = (bf16[384,256]{1,0:T(8,128)(2,1)}, bf16[384,256]{1,0:T(8,128)(2,1)S(1)}, u32[]{:S(2)}, u32[]{:S(2)}) collective-permute-start(bf16[384,256]{1,0:T(8,128)(2,1)} %param.10), channel_id=1, source_target_pairs={{0,32},{16,48},{32,64},{48,80},{64,96},{80,112},{96,128},{112,144}... | collective-permute-start | bytes 589832 | tf_op jit(solution)/shard_map/ppermute | solution.py:15
  40.4 0.9 constant_dynamic-update-slice_fusion.4
  41.3 3.9 %collective-permute-done.6 = bf16[384,256]{1,0:T(8,128)(2,1)S(1)} collective-permute-done((bf16[384,256]{1,0:T(8,128)(2,1)}, bf16[384,256]{1,0:T(8,128)(2,1)S(1)}, u32[]{:S(2)}, u32[]{:S(2)}) %collective-permute-start.6) | collective-permute-done | bytes 196640 | tf_op jit(solution)/shard_map/ppermute | solution.py:15
  45.2 0.0 copy-done.3
  45.2 17.0 %collective-permute-start.8 = (bf16[384,256]{1,0:T(8,128)(2,1)S(1)}, bf16[384,256]{1,0:T(8,128)(2,1)S(1)}, u32[]{:S(2)}, u32[]{:S(2)}) collective-permute-start(bf16[384,256]{1,0:T(8,128)(2,1)S(1)} %copy-done.3), channel_id=1, source_target_pairs={{0,16},{16,32},{32,48},{48,64},{64,80},{80,96},{96,112},{112,128},... | collective-permute-start | bytes 589832 | tf_op jit(solution)/shard_map/ppermute | solution.py:15
  62.3 0.0 collective-permute-done.7
  62.3 1.9 collective-permute-start.9
  64.2 1.8 collective-permute-done.8
  66.0 1.3 collective-permute-start.10
  67.3 0.0 copy-start.2
  67.3 0.0 collective-permute-done.3
  67.4 1.4 collective-permute-start.11
  68.8 0.9 constant_dynamic-update-slice_fusion.3
  69.7 0.0 collective-permute-done.4
  69.8 0.0 collective-permute-done.5
  69.8 0.0 copy-start.1
  69.8 3.1 %collective-permute-done.9 = bf16[384,256]{1,0:T(8,128)(2,1)S(1)} collective-permute-done((bf16[384,256]{1,0:T(8,128)(2,1)S(1)}, bf16[384,256]{1,0:T(8,128)(2,1)S(1)}, u32[]{:S(2)}, u32[]{:S(2)}) %collective-permute-start.9) | collective-permute-done | bytes 196640 | tf_op jit(solution)/shard_map/ppermute | solution.py:15
  72.9 4.7 %collective-permute-done.10 = bf16[384,256]{1,0:T(8,128)(2,1)S(1)} collective-permute-done((bf16[384,256]{1,0:T(8,128)(2,1)S(1)}, bf16[384,256]{1,0:T(8,128)(2,1)S(1)}, u32[]{:S(2)}, u32[]{:S(2)}) %collective-permute-start.10) | collective-permute-done | bytes 196640 | tf_op jit(solution)/shard_map/ppermute | solution.py:15
  77.7 4.7 %collective-permute-done.11 = bf16[384,256]{1,0:T(8,128)(2,1)S(1)} collective-permute-done((bf16[384,256]{1,0:T(8,128)(2,1)S(1)}, bf16[384,256]{1,0:T(8,128)(2,1)S(1)}, u32[]{:S(2)}, u32[]{:S(2)}) %collective-permute-start.11) | collective-permute-done | bytes 196640 | tf_op jit(solution)/shard_map/ppermute | solution.py:15
  82.4 0.0 copy-start.4
  82.5 0.0 copy-done.1
  82.5 1.1 copy-done.4
  83.5 0.0 copy-done.2
  83.5 11.1 %while.18 = (s32[]{:T(128)}, bf16[2,384,128]{1,2,0:T(8,128)(2,1)S(1)}, s32[2]{0:T(128)S(1)}, bf16[384,256]{1,0:T(8,128)(2,1)S(1)}, bf16[2688,256]{1,0:T(8,128)(2...) while((s32[]{:T(128)}, ...), condition=%wide.region_4.5_spmd.clone, body=%wide.region_1.0_spmd.clone.sunk | while | flops 537869568 | bytes 19884240 | solution.py:71
  83.5 0.6 dynamic_slice.43
  84.7 0.1 broadcast_in_dim.83
  84.8 2.0 fusion.35
  86.8 0.0 copy-start.5
  86.8 0.9 fusion.36
  87.6 0.5 copy-done.5
  88.1 0.8 fusion.37
  88.9 0.1 copy.12
  89.1 0.6 dynamic_slice.43
  90.2 0.1 broadcast_in_dim.83
  90.3 2.0 fusion.35
  92.3 0.0 copy-start.5
  92.3 0.9 fusion.36
  93.2 0.5 copy-done.5
  93.7 0.8 fusion.37
  94.4 0.1 copy.12
  94.6 0.0 copy-done
  94.6 3.1 %convolution_convert_fusion = bf16[384,5120]{1,0:T(8,128)(2,1)} fusion(bf16[384,256]{0,1:T(8,128)(2,1)S(1)} %bitcast.15, bf16[256,5120]{1,0:T(8,128)(2,1)S(1)} %copy-done), kind=kOutput, calls=%fused_computation.20 | convolution fusion | flops 1008599040 | bytes 6750208 | tf_op jit(solution)/shard_map/dot_general | solution.py:78
  97.7 0.0 reduce-scatter.2.cloned.1.call-update
  97.7 115.1 %reduce-scatter.2.cloned.1.call-done = bf16[24,5120]{1,0:T(8,128)(2,1)} async-done(((bf16[384,5120]{1,0:T(8,128)(2,1)}), bf16[24,5120]{1,0:T(8,128)(2,1)}) %reduce-scatter.2.cloned.1.call-update) | async-done | bytes 245776 | tf_op jit(solution)/shard_map/reduce_scatter | solution.py:77
  (19 shorter events, 0.3 us)
Async XLA Ops:
  6.5 88.1 %copy-start = (bf16[256,5120]{1,0:T(8,128)(2,1)S(1)}, bf16[256,5120]{1,0:T(8,128)(2,1)}, u32[]{:S(2)}) copy-start(bf16[256,5120]{1,0:T(8,128)(2,1)} %param.11) | copy-start | bytes 7864324
  6.5 38.7 %copy-start.3 = (bf16[384,256]{1,0:T(8,128)(2,1)S(1)}, bf16[384,256]{1,0:T(8,128)(2,1)}, u32[]{:S(2)}) copy-start(bf16[384,256]{1,0:T(8,128)(2,1)} %param.10) | copy-start | bytes 589828
  6.5 206.3 %reduce-scatter.2.cloned.1.call-start = ((), (), s32[]{:S(2)}) async-start(), calls=%async_computation.1 | async-start | bytes 4177920 | tf_op jit(solution)/shard_map/reduce_scatter | solution.py:77
  6.5 18.3 %collective-permute-start = (bf16[384,256]{1,0:T(8,128)(2,1)}, bf16[384,256]{1,0:T(8,128)(2,1)}, u32[]{:S(2)}, u32[]{:S(2)}) collective-permute-start(bf16[384,256]{1,0:T(8,128)(2,1)} %param.9), channel_id=1, source_target_pairs={{0,48},{16,64},{32,80},{48,96},{64,112},{80,128},{96,144},{112,160... | collective-permute-start | bytes 589832 | tf_op jit(solution)/shard_map/ppermute | solution.py:15
  11.6 15.5 %collective-permute-start.1 = (bf16[384,256]{1,0:T(8,128)(2,1)}, bf16[384,256]{1,0:T(8,128)(2,1)}, u32[]{:S(2)}, u32[]{:S(2)}) collective-permute-start(bf16[384,256]{1,0:T(8,128)(2,1)} %param.9), channel_id=1, source_target_pairs={{0,32},{16,48},{32,64},{48,80},{64,96},{80,112},{96,128},{112,144}... | collective-permute-start | bytes 589832 | tf_op jit(solution)/shard_map/ppermute | solution.py:15
  16.1 21.5 %collective-permute-start.2 = (bf16[384,256]{1,0:T(8,128)(2,1)}, bf16[384,256]{1,0:T(8,128)(2,1)S(1)}, u32[]{:S(2)}, u32[]{:S(2)}) collective-permute-start(bf16[384,256]{1,0:T(8,128)(2,1)} %param.9), channel_id=1, source_target_pairs={{0,16},{16,32},{32,48},{48,64},{64,80},{80,96},{96,112},{112,128},... | collective-permute-start | bytes 589832 | tf_op jit(solution)/shard_map/ppermute | solution.py:15
  19.9 47.5 %collective-permute-start.3 = (bf16[384,256]{1,0:T(8,128)(2,1)}, bf16[384,256]{1,0:T(8,128)(2,1)}, u32[]{:S(2)}, u32[]{:S(2)}) collective-permute-start(bf16[384,256]{1,0:T(8,128)(2,1)} %param.9), channel_id=1, source_target_pairs={{16,0},{32,16},{48,32},{64,48},{80,64},{96,80},{112,96},{128,112},... | collective-permute-start | bytes 589832 | tf_op jit(solution)/shard_map/ppermute | solution.py:15
  22.0 47.7 %collective-permute-start.4 = (bf16[384,256]{1,0:T(8,128)(2,1)}, bf16[384,256]{1,0:T(8,128)(2,1)S(1)}, u32[]{:S(2)}, u32[]{:S(2)}) collective-permute-start(bf16[384,256]{1,0:T(8,128)(2,1)} %param.9), channel_id=1, source_target_pairs={{32,0},{48,16},{64,32},{80,48},{96,64},{112,80},{128,96},{144,112}... | collective-permute-start | bytes 589832 | tf_op jit(solution)/shard_map/ppermute | solution.py:15
  24.8 44.9 %collective-permute-start.5 = (bf16[384,256]{1,0:T(8,128)(2,1)}, bf16[384,256]{1,0:T(8,128)(2,1)S(1)}, u32[]{:S(2)}, u32[]{:S(2)}) collective-permute-start(bf16[384,256]{1,0:T(8,128)(2,1)} %param.9), channel_id=1, source_target_pairs={{48,0},{64,16},{80,32},{96,48},{112,64},{128,80},{144,96},{160,112... | collective-permute-start | bytes 589832 | tf_op jit(solution)/shard_map/ppermute | solution.py:15
  27.1 18.1 %collective-permute-start.6 = (bf16[384,256]{1,0:T(8,128)(2,1)}, bf16[384,256]{1,0:T(8,128)(2,1)S(1)}, u32[]{:S(2)}, u32[]{:S(2)}) collective-permute-start(bf16[384,256]{1,0:T(8,128)(2,1)} %param.10), channel_id=1, source_target_pairs={{0,48},{16,64},{32,80},{48,96},{64,112},{80,128},{96,144},{112,160... | collective-permute-start | bytes 589832 | tf_op jit(solution)/shard_map/ppermute | solution.py:15
  37.7 24.6 %collective-permute-start.7 = (bf16[384,256]{1,0:T(8,128)(2,1)}, bf16[384,256]{1,0:T(8,128)(2,1)S(1)}, u32[]{:S(2)}, u32[]{:S(2)}) collective-permute-start(bf16[384,256]{1,0:T(8,128)(2,1)} %param.10), channel_id=1, source_target_pairs={{0,32},{16,48},{32,64},{48,80},{64,96},{80,112},{96,128},{112,144}... | collective-permute-start | bytes 589832 | tf_op jit(solution)/shard_map/ppermute | solution.py:15
  45.2 20.8 %collective-permute-start.8 = (bf16[384,256]{1,0:T(8,128)(2,1)S(1)}, bf16[384,256]{1,0:T(8,128)(2,1)S(1)}, u32[]{:S(2)}, u32[]{:S(2)}) collective-permute-start(bf16[384,256]{1,0:T(8,128)(2,1)S(1)} %copy-done.3), channel_id=1, source_target_pairs={{0,16},{16,32},{32,48},{48,64},{64,80},{80,96},{96,112},{112,128},... | collective-permute-start | bytes 589832 | tf_op jit(solution)/shard_map/ppermute | solution.py:15
  62.3 10.7 %collective-permute-start.9 = (bf16[384,256]{1,0:T(8,128)(2,1)S(1)}, bf16[384,256]{1,0:T(8,128)(2,1)S(1)}, u32[]{:S(2)}, u32[]{:S(2)}) collective-permute-start(bf16[384,256]{1,0:T(8,128)(2,1)S(1)} %copy-done.3), channel_id=1, source_target_pairs={{16,0},{32,16},{48,32},{64,48},{80,64},{96,80},{112,96},{128,112},... | collective-permute-start | bytes 589832 | tf_op jit(solution)/shard_map/ppermute | solution.py:15
  66.0 11.6 %collective-permute-start.10 = (bf16[384,256]{1,0:T(8,128)(2,1)S(1)}, bf16[384,256]{1,0:T(8,128)(2,1)S(1)}, u32[]{:S(2)}, u32[]{:S(2)}) collective-permute-start(bf16[384,256]{1,0:T(8,128)(2,1)S(1)} %copy-done.3), channel_id=1, source_target_pairs={{32,0},{48,16},{64,32},{80,48},{96,64},{112,80},{128,96},{144,112}... | collective-permute-start | bytes 589832 | tf_op jit(solution)/shard_map/ppermute | solution.py:15
  67.3 16.2 %copy-start.2 = (bf16[384,256]{1,0:T(8,128)(2,1)S(1)}, bf16[384,256]{1,0:T(8,128)(2,1)}, u32[]{:S(2)}) copy-start(bf16[384,256]{1,0:T(8,128)(2,1)} %param.8) | copy-start | bytes 589828
  67.4 15.1 %collective-permute-start.11 = (bf16[384,256]{1,0:T(8,128)(2,1)S(1)}, bf16[384,256]{1,0:T(8,128)(2,1)S(1)}, u32[]{:S(2)}, u32[]{:S(2)}) collective-permute-start(bf16[384,256]{1,0:T(8,128)(2,1)S(1)} %copy-done.3), channel_id=1, source_target_pairs={{48,0},{64,16},{80,32},{96,48},{112,64},{128,80},{144,96},{160,112... | collective-permute-start | bytes 589832 | tf_op jit(solution)/shard_map/ppermute | solution.py:15
  69.8 12.7 %copy-start.1 = (bf16[2688,256]{1,0:T(8,128)(2,1)}, bf16[2688,256]{1,0:T(8,128)(2,1)S(1)}, u32[]{:S(2)}) copy-start(bf16[2688,256]{1,0:T(8,128)(2,1)S(1)} %constant_dynamic-update-slice_fusion.1) | copy-start | bytes 4128772
  82.4 1.1 copy-start.4
  86.8 1.3 copy-start.5
  92.3 1.3 copy-start.5
Sparse Core Ops, SparseCore 0:
  97.9 114.9 reduce-scatter.1
where the time goes:
time: 220 us
  waiting for transfers between devices  133 us (60%)
  starting transfers between devices  51.9 us (24%)
  between operations  14.3 us (6%)
  matrix products  8.63 us (4%)
  local copies, waits for them, and re-layouts  7.59 us (3%)
  other arithmetic  2.57 us (1%)
    reduce_scatter x1, waiting for transfers between devices, local(): lax.psum_scatter(jnp.dot(attended, out_weight, preferred_element_type=jnp...  115 us
    ppermute x12, starting transfers between devices, passed_along(): lax.ppermute(value, axis, [(source, source + steps) for source in range(f...  51.9 us
    ppermute x12, waiting for transfers between devices, passed_along(): lax.ppermute(value, axis, [(source, source + steps) for source in range(f...  18.3 us
    unnamed x22, local copies, waits for them, and re-layouts  4.96 us
  transfers between devices with their start and end apart: 13, of which 6 were waited for; matrix products, arithmetic and copies ran while one was open for 2% of the time, Pallas kernels for 0%

commit v1 on v0

v1 whole, which is shorter than its diff:
```python
import functools
import math

import jax
import jax.numpy as jnp
from jax import lax
from jax.experimental import pallas as pl
from jax.experimental.pallas import tpu as pltpu
from jax.sharding import PartitionSpec as P

MESH = pl.DeviceIdType.MESH
HD = 128
TILE = 384
ROW = 4
NZ = 8
NX = 4
OWN = 24
HALF = 192
D = 5120
CHUNKS = 8
CW = D // CHUNKS
MASKED = 1e30
FACTOR = math.log2(math.e) / math.sqrt(HD)
LAG2, LAG3, LAG4 = 2, 4, 7


def body(
    q_hbm, k_hbm, v_hbm, w_hbm, nb_ref, ct_ref, out_ref,
    q_win, k_win, v_win, bias_src, bias_win, m_ref, l_ref, acc_ref, o_buf, att, w_buf,
    part, got1, got2, got3, send3, summed, send4, got4,
    s_dir, r_q, r_k, r_v, r_b, s_fwd, s_o, r_o, s_w, r_w, s1, s2, s3, s4, r1, r2, r3, r4,
):
    ctx = lax.axis_index("ctx")
    head = lax.axis_index("head")
    z, y = ctx // ROW, ctx % ROW
    yh, x, k = head // 8, (head // 2) % NX, head % 2

    def dev(zz, yy, kk):
        return {"ctx": zz * ROW + yy, "head": yh * 8 + x * 2 + kk}

    def xdev(xx):
        return {"ctx": ctx, "head": yh * 8 + xx * 2 + k}

    partner = {"ctx": ctx, "head": (1 - yh) * 8 + x * 2 + k}
    sibling = dev(z, y, 1 - k)
    right, left = (x + 1) % NX, (x + NX - 1) % NX

    w_own = pltpu.make_async_copy(w_hbm, w_buf.at[k], r_w.at[k])
    w_own.start()

    barrier = pltpu.get_barrier_semaphore()
    greeted = [sibling, xdev(right), xdev(left), partner]
    for step in range(1, ROW):
        for kk in range(2):
            greeted.append(dev(z, (y + step) % ROW, kk))
    for step in (1, NZ - 1):
        for kk in range(2):
            greeted.append(dev((z + step) % NZ, y, kk))
    for target in greeted:
        pl.semaphore_signal(barrier, inc=1, device_id=target, device_id_type=MESH)

    rows = lax.broadcasted_iota(jnp.int32, (8, HD), 0)
    bias = jnp.zeros((8, HD), jnp.float32)
    for o in range(7):
        allowed = jnp.int32(0)
        for i in range(7):
            hit = (nb_ref[0, i] == ctx + (o - 3)) & (i < ct_ref[0])
            allowed = allowed + hit.astype(jnp.int32)
        value = jnp.where(allowed > 0, jnp.float32(0), jnp.float32(MASKED))
        bias = jnp.where(rows == o, value, bias)
    bias_src[...] = bias
    m_ref[...] = jnp.full(m_ref.shape, -1e29, jnp.float32)
    l_ref[...] = jnp.zeros(l_ref.shape, jnp.float32)
    acc_ref[...] = jnp.zeros(acc_ref.shape, jnp.float32)

    pl.semaphore_wait(barrier, len(greeted))

    kd, yq = y // 2, y % 2

    def direct(i, remote):
        cols = pl.ds(i * HD, HD)
        moves = (
            (q_hbm.at[:, cols], q_win.at[yq], r_q.at[yq]),
            (bias_src, bias_win.at[yq], r_b.at[yq]),
            (k_hbm.at[:, cols], k_win.at[3 + yq], r_k.at[3 + yq]),
            (v_hbm.at[:, cols], v_win.at[3 + yq], r_v.at[3 + yq]),
        )
        out = []
        for n, (src, dst, sem) in enumerate(moves):
            if remote:
                out.append(
                    pltpu.make_async_remote_copy(
                        src, dst, s_dir.at[i, n], sem,
                        device_id=dev(z, 2 * k + i, kd), device_id_type=MESH,
                    )
                )
            else:
                out.append(pltpu.make_async_copy(src, dst, sem))
        return out

    for i in range(2):
        @pl.when(2 * k + i != y)
        def _(i=i):
            for copy in direct(i, True):
                copy.start()

    for i in range(2):
        @pl.when(2 * k + i == y)
        def _(i=i):
            for copy in direct(i, False):
                copy.start()

    w_sib = pltpu.make_async_remote_copy(
        w_hbm, w_buf.at[k], s_w, r_w.at[k], device_id=sibling, device_id_type=MESH
    )
    w_sib.start()

    def slot(a):
        return a + k * (7 - 2 * a)

    z_out, z_in = z - 1 + 2 * k, z + 1 - 2 * k
    has_out = (z_out >= 0) & (z_out < NZ)
    has_in = (z_in >= 0) & (z_in < NZ)

    def forward(a, n, b, target):
        src, dst = slot(a), slot(b)
        return [
            pltpu.make_async_remote_copy(
                win.at[src], win.at[dst], s_fwd.at[2 * n + j], sems.at[dst],
                device_id=target, device_id_type=MESH,
            )
            for j, (win, sems) in enumerate(((k_win, r_k), (v_win, r_v)))
        ]

    z_o, z_i = (z_out + NZ) % NZ, (z_in + NZ) % NZ
    plan = (
        (3, 0, 5, dev(z_o, y, 1 - k), has_out),
        (3, 1, 7, dev(z_o, y, k), has_out),
        (3, 2, 1, sibling, None),
        (4, 3, 0, dev(z_i, y, k), has_in),
        (4, 4, 6, dev(z_o, y, 1 - k), has_out),
        (4, 5, 2, sibling, None),
    )

    def arrived(sems, win, s):
        pltpu.make_async_copy(win.at[s], win.at[s], sems.at[s]).wait()

    for a in (3, 4):
        for j, (win, sems) in enumerate(((k_win, r_k), (v_win, r_v))):
            arrived(sems, win, slot(a))
            for first, n, b, target, there in plan:
                if first != a:
                    continue
                copy = forward(a, n, b, target)[j]
                if there is None:
                    copy.start()
                else:
                    pl.when(there)(copy.start)

    for i in range(2):
        arrived(r_q, q_win, i)
        arrived(r_b, bias_win, i)

    def unit(i, s):
        scores = lax.dot_general(
            q_win[i], k_win[s], (((1,), (1,)), ((), ())), preferred_element_type=jnp.float32
        )
        off = bias_win[i, pl.ds(s - i, 1), :][:, :1]
        before = m_ref[i]
        now = jnp.maximum(before, jnp.max(scores, axis=1, keepdims=True) - off)
        weights = jnp.exp2((scores - (now + off)) * FACTOR)
        alpha = jnp.exp2((before - now) * FACTOR)
        m_ref[i] = now
        l_ref[i] = alpha * l_ref[i] + jnp.sum(weights, axis=1, keepdims=True)
        acc_ref[i] = alpha * acc_ref[i] + jnp.dot(
            weights.astype(jnp.bfloat16), v_win[s], preferred_element_type=jnp.float32
        )

    def both(j, carry):
        s = slot(3 + j - (j // 4) * (2 * j - 3))

        @pl.when((j < 4) | has_out)
        def _():
            @pl.when(j >= 2)
            def _():
                arrived(r_k, k_win, s)
                arrived(r_v, v_win, s)

            unit(0, s)
            unit(1, s)

        return carry

    lax.fori_loop(0, 6, both, 0)

    def single(j, carry):
        s = slot(7 * j)
        i = j + k * (1 - 2 * j)

        @pl.when(((j == 0) & has_out) | ((j == 1) & has_in))
        def _():
            arrived(r_k, k_win, s)
            arrived(r_v, v_win, s)
            unit(i, s)

        return carry

    lax.fori_loop(0, 2, single, 0)

    def home(i, r, remote):
        src, dst = o_buf.at[i, r], att.at[y]
        if remote:
            return pltpu.make_async_remote_copy(
                src, dst, s_o.at[i, r], r_o.at[y],
                device_id=dev(z, 2 * k + i, r), device_id_type=MESH,
            )
        return pltpu.make_async_copy(src, dst, r_o.at[y])

    for i in range(2):
        mixed = acc_ref[i] * (1.0 / l_ref[i])
        for r in range(2):
            pieces = [
                mixed[OWN * (8 * h + 2 * xx + r) : OWN * (8 * h + 2 * xx + r + 1)]
                for xx in range(NX)
                for h in range(2)
            ]
            o_buf[i, r] = jnp.concatenate(pieces, axis=0).astype(jnp.bfloat16)
            here = (2 * k + i == y) & (k == r)
            pl.when(jnp.logical_not(here))(home(i, r, True).start)
            pl.when(here)(home(i, r, False).start)

    w_own.wait()
    pltpu.make_async_copy(w_buf.at[1 - k], w_buf.at[1 - k], r_w.at[1 - k]).wait()
    for j in range(ROW):
        arrived(r_o, att, j)

    low = jnp.concatenate([att[0], att[1]], axis=1)
    high = jnp.concatenate([att[2], att[3]], axis=1)

    def toward(n):
        return (right, left) if n % 2 == 0 else (left, right)

    def copy1(n):
        ahead, behind = toward(n)
        far = (x + 2) % NX
        return (
            pltpu.make_async_remote_copy(
                part.at[n, far], got1.at[n], s1.at[n], r1.at[n],
                device_id=xdev(ahead), device_id_type=MESH,
            ),
            pltpu.make_async_remote_copy(
                part.at[n, behind], got2.at[n], s2.at[n], r2.at[n],
                device_id=xdev(behind), device_id_type=MESH,
            ),
        )

    def copy3(n):
        return pltpu.make_async_remote_copy(
            send3.at[n], got3.at[n], s3.at[n], r3.at[n],
            device_id=xdev(toward(n)[0]), device_id_type=MESH,
        )

    def copy4(n):
        return pltpu.make_async_remote_copy(
            send4.at[n], got4.at[n], s4.at[n], r4.at[n],
            device_id=partner, device_id_type=MESH,
        )

    def stage1(n):
        cols = slice(n * CW, (n + 1) * CW)
        total = jnp.dot(low, w_buf[0, :, cols], preferred_element_type=jnp.float32)
        total = total + jnp.dot(high, w_buf[1, :, cols], preferred_element_type=jnp.float32)
        part[n] = total.astype(jnp.bfloat16).reshape(NX, 2 * OWN, CW)
        for copy in copy1(n):
            copy.start()

    def stage2(n):
        copy1(n)[0].wait_recv()
        own = part[n, toward(n)[0]].astype(jnp.float32)
        send3[n] = (own + got1[n].astype(jnp.float32)).astype(jnp.bfloat16)
        copy3(n).start()

    def stage3(n):
        copy1(n)[1].wait_recv()
        copy3(n).wait_recv()
        total = part[n, x].astype(jnp.float32) + got2[n].astype(jnp.float32)
        total = total + got3[n].astype(jnp.float32)
        summed[n] = total.reshape(2, OWN, CW)
        send4[n] = summed[n, 1 - yh].astype(jnp.bfloat16)
        copy4(n).start()

    def stage4(n):
        copy4(n).wait_recv()
        total = summed[n, yh] + got4[n].astype(jnp.float32)
        out_ref[:, n * CW : (n + 1) * CW] = total.astype(jnp.bfloat16)

    for step in range(CHUNKS + LAG4):
        for lag, stage in ((0, stage1), (LAG2, stage2), (LAG3, stage3), (LAG4, stage4)):
            if 0 <= step - lag < CHUNKS:
                stage(step - lag)

    for i in range(2):
        @pl.when(2 * k + i != y)
        def _(i=i):
            for copy in direct(i, True):
                copy.wait_send()
    for a, n, b, target, there in plan:
        for copy in forward(a, n, b, target):
            if there is None:
                copy.wait_send()
            else:
                pl.when(there)(copy.wait_send)
    w_sib.wait_send()
    for i in range(2):
        for r in range(2):
            here = (2 * k + i == y) & (k == r)
            pl.when(jnp.logical_not(here))(home(i, r, True).wait_send)
    for n in range(CHUNKS):
        for copy in copy1(n):
            copy.wait_send()
        copy3(n).wait_send()
        copy4(n).wait_send()


def local(queries, keys, values, out_weight, neighbours, counts):
    bf16, f32 = jnp.bfloat16, jnp.float32
    dma = pltpu.SemaphoreType.DMA
    window = pltpu.VMEM((8, TILE, HD), bf16)
    ring = pltpu.VMEM((CHUNKS, 2 * OWN, CW), bf16)
    anywhere = pl.BlockSpec(memory_space=pl.ANY)
    scalars = pl.BlockSpec(memory_space=pltpu.SMEM)
    return pl.pallas_call(
        body,
        out_shape=jax.ShapeDtypeStruct((OWN, D), bf16),
        in_specs=[anywhere] * 4 + [scalars] * 2,
        out_specs=pl.BlockSpec(memory_space=pltpu.VMEM),
        scratch_shapes=[
            pltpu.VMEM((2, TILE, HD), bf16), window, window,
            pltpu.VMEM((8, HD), f32), pltpu.VMEM((2, 8, HD), f32),
            pltpu.VMEM((2, TILE, 1), f32), pltpu.VMEM((2, TILE, 1), f32),
            pltpu.VMEM((2, TILE, HD), f32),
            pltpu.VMEM((2, 2, HALF, HD), bf16), pltpu.VMEM((ROW, HALF, HD), bf16),
            pltpu.VMEM((2, 2 * HD, D), bf16),
            pltpu.VMEM((CHUNKS, NX, 2 * OWN, CW), bf16), ring, ring, ring, ring,
            pltpu.VMEM((CHUNKS, 2, OWN, CW), f32),
            pltpu.VMEM((CHUNKS, OWN, CW), bf16), pltpu.VMEM((CHUNKS, OWN, CW), bf16),
            dma((2, 4)), dma((2,)), dma((8,)), dma((8,)), dma((2,)), dma((12,)),
            dma((2, 2)), dma((ROW,)), dma, dma((2,)),
        ] + [dma((CHUNKS,))] * 8,
        compiler_params=pltpu.CompilerParams(
            collective_id=0, has_side_effects=True, vmem_limit_bytes=48 << 20
        ),
        name="tile_attention",
    )(queries, keys, values, out_weight, neighbours, counts)


def solution(mesh):
    placed = (
        P("ctx", "head"),
        P("ctx", "head"),
        P("ctx", "head"),
        P("head", None),
        P("ctx", None),
        P("ctx"),
    )
    return jax.shard_map(
        local, mesh=mesh, in_specs=placed, out_specs=P(("ctx", "head"), None), check_vma=False
    )
```

time: 220 us -> 75.6 us (0.34)
  waiting for transfers between devices: 133 us -> 0 us
  Pallas kernels: 0 us -> 68.8 us
  starting transfers between devices: 51.9 us -> 0 us
  between operations: 14.3 us -> 0.67 us
  matrix products: 8.63 us -> 0 us
  other arithmetic: 2.57 us -> 0 us
    reduce_scatter x1 -> x0, waiting for transfers between devices: 115 us -> none  [local(): lax.psum_scatter(jnp.dot(attended, out_weight, preferred_element_type=jnp...]
    pallas_call x0 -> x1, Pallas kernels: none -> 68.8 us  [local(): pl.pallas_call(body, out_shape=jax.ShapeDtypeStruct((OWN, D), bf16), in_s...]
    ppermute x12 -> x0, starting transfers between devices: 51.9 us -> none  [passed_along(): lax.ppermute(value, axis, [(source, source + steps) for source in range(f...]
    ppermute x12 -> x0, waiting for transfers between devices: 18.3 us -> none  [passed_along(): lax.ppermute(value, axis, [(source, source + steps) for source in range(f...]
    dot_general x5 -> x0, matrix products: 8.63 us -> none  [the longest x2 4.02 us: one_head(): jnp.einsum('qd,kd->qk', q_head, k_head, preferred_element_type=jnp.float32)]
    unnamed x22 -> x11, local copies, waits for them, and re-layouts: 4.96 us -> 5.86 us
  transfers between devices with their start and end apart: 13 -> 0, of which waited for: 6 -> 0; matrix products, arithmetic and copies ran while one was open for 2% -> 0% of each run, Pallas kernels for 0% -> 0%
where the time goes in v1:
time: 75.6 us; the launch traced here: 75.4 us
  Pallas kernels  68.8 us (91%)
  local copies, waits for them, and re-layouts  5.86 us (8%)
    pallas_call x1, Pallas kernels, local(): pl.pallas_call(body, out_shape=jax.ShapeDtypeStruct((OWN, D), bf16), in_s...  68.8 us
    unnamed x11, local copies, waits for them, and re-layouts  5.86 us

profile of v1, /device:TPU:8, one launch (start us, length us, event | category | flops | bytes accessed | tf_op | source)
XLA Modules:
  0.0 75.4 jit_solution(7390485256352689337)
XLA Ops:
  0.7 0.0 copy-start
  0.7 1.7 %copy-done = bf16[256,5120]{1,0:T(8,128)(2,1)S(1)} copy-done((bf16[256,5120]{1,0:T(8,128)(2,1)S(1)}, bf16[256,5120]{1,0:T(8,128)(2,1)}, u32[]{:S(2)}) %copy-start) | copy-done | bytes 2621464
  2.4 0.0 copy-start.1
  2.4 0.9 %copy-done.1 = bf16[384,256]{1,0:T(8,128)(2,1)S(1)} copy-done((bf16[384,256]{1,0:T(8,128)(2,1)S(1)}, bf16[384,256]{1,0:T(8,128)(2,1)}, u32[]{:S(2)}) %copy-start.1) | copy-done | bytes 196632
  3.3 0.0 copy-start.2
  3.3 0.9 %copy-done.2 = bf16[384,256]{1,0:T(8,128)(2,1)S(1)} copy-done((bf16[384,256]{1,0:T(8,128)(2,1)S(1)}, bf16[384,256]{1,0:T(8,128)(2,1)}, u32[]{:S(2)}) %copy-start.2) | copy-done | bytes 196632
  4.2 0.0 copy-start.3
  4.2 0.9 %copy-done.3 = bf16[384,256]{1,0:T(8,128)(2,1)S(1)} copy-done((bf16[384,256]{1,0:T(8,128)(2,1)S(1)}, bf16[384,256]{1,0:T(8,128)(2,1)}, u32[]{:S(2)}) %copy-start.3) | copy-done | bytes 196632
  5.2 0.0 copy-start.4
  5.2 0.7 copy-done.4
  5.8 68.8 %tile_attention.1 = bf16[24,5120]{1,0:T(8,128)(2,1)S(1)} custom-call(bf16[384,256]{1,0:T(8,128)(2,1)S(1)} %copy-done.1, bf16[384,256]{1,0:T(8,128)(2,1)S(1)} %copy-done.2, bf16[384,256]{1,0:T(8,128)(2,1)S(1)} %copy-done.3, bf16[256,5120]{1,0:T(8,128)(2,1)S(1)} %copy-done, s32[1,7]{1,0:T(1,128)S(1)} %copy-done.4, s32[1]{0:T(128)S(6)} %copy.8.ct_ref), custom_call_target="tpu_custom_call" | custom-call | tf_op jit(solution)/shard_map/tile_attention/pallas_call | solution.py:332
  74.7 0.7 copy.9
Async XLA Ops:
  0.7 1.7 %copy-start = (bf16[256,5120]{1,0:T(8,128)(2,1)S(1)}, bf16[256,5120]{1,0:T(8,128)(2,1)}, u32[]{:S(2)}) copy-start(bf16[256,5120]{1,0:T(8,128)(2,1)} %w_hbm.1) | copy-start | bytes 7864324
  2.4 0.9 %copy-start.1 = (bf16[384,256]{1,0:T(8,128)(2,1)S(1)}, bf16[384,256]{1,0:T(8,128)(2,1)}, u32[]{:S(2)}) copy-start(bf16[384,256]{1,0:T(8,128)(2,1)} %q_hbm.1) | copy-start | bytes 589828
  3.3 0.9 %copy-start.2 = (bf16[384,256]{1,0:T(8,128)(2,1)S(1)}, bf16[384,256]{1,0:T(8,128)(2,1)}, u32[]{:S(2)}) copy-start(bf16[384,256]{1,0:T(8,128)(2,1)} %k_hbm.1) | copy-start | bytes 589828
  4.2 0.9 %copy-start.3 = (bf16[384,256]{1,0:T(8,128)(2,1)S(1)}, bf16[384,256]{1,0:T(8,128)(2,1)}, u32[]{:S(2)}) copy-start(bf16[384,256]{1,0:T(8,128)(2,1)} %v_hbm.1) | copy-start | bytes 589828
  5.2 0.7 copy-start.4

commit v2 on v1

v2 whole, which is shorter than its diff:
```python
import functools
import math

import jax
import jax.numpy as jnp
from jax import lax
from jax.experimental import pallas as pl
from jax.experimental.pallas import tpu as pltpu
from jax.sharding import PartitionSpec as P

MESH = pl.DeviceIdType.MESH
HD = 128
TILE = 384
ROW = 4
NZ = 8
NX = 4
OWN = 24
HALF = 192
D = 5120
CHUNKS = 9
CW = 512
YW = 512
YH = YW // 2
XCOLS = CHUNKS * CW
MASKED = 1e30
FACTOR = math.log2(math.e) / math.sqrt(HD)
LAG2, LAG3, LAG4 = 2, 5, 9
Y2, Y3, Y4 = CHUNKS + LAG2 - 1, CHUNKS + LAG3 - 1, CHUNKS + LAG4 - 2
ORDER = (2, 1, 0, 3)


def body(
    q_hbm, k_hbm, v_hbm, w_hbm, nb_hbm, ct_ref, out_ref,
    nb_ref, q_win, k_win, v_win, bias_src, bias_win, score, weight, m_ref, l_ref, acc_ref,
    o_buf, att, w_buf,
    part, got1, got2, got3, send3, summed, send4, got4,
    part_y, send_y, got_y, half_y, got1_y, got2_y, got3_y, send3_y,
    s_dir, r_q, r_k, r_v, r_b, s_fwd, s_o, r_o, s_w, r_w, s_nb,
    s1, s2, s3, s4, r1, r2, r3, r4, s_y, r_y, s1_y, s2_y, s3_y, r1_y, r2_y, r3_y,
):
    ctx = lax.axis_index("ctx")
    head = lax.axis_index("head")
    z, y = ctx // ROW, ctx % ROW
    yh, x, k = head // 8, (head // 2) % NX, head % 2

    def dev(zz, yy, kk):
        return {"ctx": zz * ROW + yy, "head": yh * 8 + x * 2 + kk}

    def xdev(xx):
        return {"ctx": ctx, "head": yh * 8 + xx * 2 + k}

    partner = {"ctx": ctx, "head": (1 - yh) * 8 + x * 2 + k}
    sibling = dev(z, y, 1 - k)
    right, left = (x + 1) % NX, (x + NX - 1) % NX

    w_own = pltpu.make_async_copy(w_hbm, w_buf.at[k], r_w.at[k])
    w_own.start()
    listing = pltpu.make_async_copy(nb_hbm, nb_ref, s_nb)
    listing.start()

    barrier = pltpu.get_barrier_semaphore()
    greeted = [sibling, xdev(right), xdev(left), partner]
    for step in range(1, ROW):
        for kk in range(2):
            greeted.append(dev(z, (y + step) % ROW, kk))
    for step in (1, NZ - 1):
        for kk in range(2):
            greeted.append(dev((z + step) % NZ, y, kk))
    for target in greeted:
        pl.semaphore_signal(barrier, inc=1, device_id=target, device_id_type=MESH)

    z_out, z_in = z - 1 + 2 * k, z + 1 - 2 * k
    has_out = (z_out >= 0) & (z_out < NZ)
    has_in = (z_in >= 0) & (z_in < NZ)
    z_o, z_i = (z_out + NZ) % NZ, (z_in + NZ) % NZ

    def slot(a):
        return a + k * (7 - 2 * a)

    for side, tiles in ((has_out, (0, 1, 2)), (has_in, (7,))):
        @pl.when(jnp.logical_not(side))
        def _(tiles=tiles):
            for a in tiles:
                k_win[slot(a)] = jnp.zeros((TILE, HD), jnp.bfloat16)
                v_win[slot(a)] = jnp.zeros((TILE, HD), jnp.bfloat16)

    listing.wait()
    rows = lax.broadcasted_iota(jnp.int32, (8, HD), 0)
    bias = jnp.zeros((8, HD), jnp.float32)
    for o in range(7):
        allowed = jnp.int32(0)
        for i in range(7):
            hit = (nb_ref[0, i] == ctx + (o - 3)) & (i < ct_ref[0])
            allowed = allowed + hit.astype(jnp.int32)
        value = jnp.where(allowed > 0, jnp.float32(0), jnp.float32(MASKED))
        bias = jnp.where(rows == o, value, bias)
    bias_src[...] = bias
    m_ref[...] = jnp.full(m_ref.shape, -MASKED, jnp.float32)
    l_ref[...] = jnp.zeros(l_ref.shape, jnp.float32)

    pl.semaphore_wait(barrier, len(greeted))

    kd, yq = y // 2, y % 2

    def direct(i, n, remote):
        cols = pl.ds(i * HD, HD)
        src, dst, sem = (
            (q_hbm.at[:, cols], q_win.at[yq], r_q.at[yq]),
            (bias_src, bias_win.at[yq], r_b.at[yq]),
            (k_hbm.at[:, cols], k_win.at[3 + yq], r_k.at[3 + yq]),
            (v_hbm.at[:, cols], v_win.at[3 + yq], r_v.at[3 + yq]),
        )[n]
        if remote:
            return pltpu.make_async_remote_copy(
                src, dst, s_dir.at[i, n], sem,
                device_id=dev(z, 2 * k + i, kd), device_id_type=MESH,
            )
        return pltpu.make_async_copy(src, dst, sem)

    for n in ORDER:
        for i in range(2):
            pl.when(2 * k + i != y)(lambda i=i, n=n: direct(i, n, True).start())
            pl.when(2 * k + i == y)(lambda i=i, n=n: direct(i, n, False).start())

    w_sib = pltpu.make_async_remote_copy(
        w_hbm, w_buf.at[k], s_w, r_w.at[k], device_id=sibling, device_id_type=MESH
    )
    w_sib.start()

    windows = ((k_win, r_k), (v_win, r_v))
    plan = (
        (3, 0, 1, sibling, None),
        (3, 1, 5, dev(z_o, y, 1 - k), has_out),
        (4, 2, 2, sibling, None),
        (4, 3, 0, dev(z_i, y, k), has_in),
        (4, 4, 6, dev(z_o, y, 1 - k), has_out),
        (2, 5, 0, sibling, has_out),
    )

    def forward(n, b, a, target, j):
        win, sems = windows[j]
        return pltpu.make_async_remote_copy(
            win.at[slot(a)], win.at[slot(b)], s_fwd.at[j, n], sems.at[slot(b)],
            device_id=target, device_id_type=MESH,
        )

    def arrived(sems, win, s):
        pltpu.make_async_copy(win.at[s], win.at[s], sems.at[s]).wait()

    def take(a, j):
        arrived(windows[j][1], windows[j][0], slot(a))
        for source, n, b, target, there in plan:
            if source != a:
                continue
            if there is None or a == 2:
                forward(n, b, a, target, j).start()
            else:
                pl.when(there)(lambda: forward(n, b, a, target, j).start())

    def lanes(s):
        return pl.ds(pl.multiple_of(s * TILE, TILE), TILE)

    def scores(i, s):
        raw = lax.dot_general(
            q_win[i], k_win[s], (((1,), (1,)), ((), ())), preferred_element_type=jnp.float32
        )
        score[i, :, lanes(s)] = raw
        high = jnp.maximum(jnp.maximum(raw[:, :HD], raw[:, HD : 2 * HD]), raw[:, 2 * HD :])
        m_ref[i] = jnp.maximum(m_ref[i], high - bias_win[i, pl.ds(s - i, 1), :])

    def weigh(i, j):
        off = m_ref[i][:, :1] + bias_win[i, pl.ds(j, 1), :][:, :1]
        exact = jnp.exp2((score[i, :, lanes(i + j)] - off) * FACTOR)
        weight[i, :, lanes(i + j)] = exact.astype(jnp.bfloat16)
        l_ref[i] = l_ref[i] + (exact[:, :HD] + exact[:, HD : 2 * HD] + exact[:, 2 * HD :])

    def product(i, s):
        acc_ref[i] = acc_ref[i] + jnp.dot(
            weight[i, :, lanes(s)], v_win[s], preferred_element_type=jnp.float32
        )

    def mirrored(i):
        return i + k * (1 - 2 * i)

    take(3, 0)
    take(4, 0)
    for i in range(2):
        arrived(r_q, q_win, i)
        arrived(r_b, bias_win, i)

    def near_scores(j, carry):
        s = slot(3 + j)

        @pl.when(j >= 2)
        def _():
            arrived(r_k, k_win, s)

        scores(0, s)
        scores(1, s)
        return carry

    lax.fori_loop(0, 4, near_scores, 0)

    @pl.when(has_out)
    def _():
        take(2, 0)
        arrived(r_k, k_win, slot(1))

    def far_scores(j, carry):
        s = slot(2 - j)
        scores(0, s)
        scores(1, s)
        return carry

    lax.fori_loop(0, 2, far_scores, 0)

    @pl.when(has_out)
    def _():
        arrived(r_k, k_win, slot(0))

    @pl.when(has_in)
    def _():
        arrived(r_k, k_win, slot(7))

    def last_scores(j, carry):
        scores(mirrored(j), slot(7 * j))
        return carry

    lax.fori_loop(0, 2, last_scores, 0)

    take(3, 1)
    for i in range(2):
        m_ref[i] = jnp.broadcast_to(jnp.max(m_ref[i], axis=1, keepdims=True), (TILE, HD))

    def weigh_both(j, carry):
        weigh(0, j)
        weigh(1, j)
        return carry

    lax.fori_loop(0, 3, weigh_both, 0)
    take(4, 1)
    lax.fori_loop(3, 7, weigh_both, 0)

    arrived(r_v, v_win, slot(5))
    arrived(r_v, v_win, slot(6))
    first = 3 - 2 * k
    own = pl.ds(pl.multiple_of(first * TILE, TILE), ROW * TILE)
    near_v = v_win[pl.ds(first, ROW)].reshape(ROW * TILE, HD)
    for i in range(2):
        acc_ref[i] = jnp.dot(weight[i, :, own], near_v, preferred_element_type=jnp.float32)

    @pl.when(has_out)
    def _():
        take(2, 1)
        arrived(r_v, v_win, slot(1))

    def far_products(j, carry):
        s = slot(2 - j)
        product(0, s)
        product(1, s)
        return carry

    lax.fori_loop(0, 2, far_products, 0)

    @pl.when(has_out)
    def _():
        arrived(r_v, v_win, slot(0))

    @pl.when(has_in)
    def _():
        arrived(r_v, v_win, slot(7))

    def last_products(j, carry):
        product(mirrored(j), slot(7 * j))
        return carry

    lax.fori_loop(0, 2, last_products, 0)

    def home(i, r, remote):
        src, dst = o_buf.at[i, r], att.at[y]
        if remote:
            return pltpu.make_async_remote_copy(
                src, dst, s_o.at[i, r], r_o.at[y],
                device_id=dev(z, 2 * k + i, r), device_id_type=MESH,
            )
        return pltpu.make_async_copy(src, dst, r_o.at[y])

    for i in range(2):
        mixed = acc_ref[i] * (1.0 / jnp.sum(l_ref[i], axis=1, keepdims=True))
        for r in range(2):
            pieces = [
                mixed[OWN * (8 * h + 2 * xx + r) : OWN * (8 * h + 2 * xx + r + 1)]
                for xx in range(NX)
                for h in range(2)
            ]
            o_buf[i, r] = jnp.concatenate(pieces, axis=0).astype(jnp.bfloat16)
            here = (2 * k + i == y) & (k == r)
            pl.when(jnp.logical_not(here))(lambda: home(i, r, True).start())
            pl.when(here)(lambda: home(i, r, False).start())

    w_own.wait()
    pltpu.make_async_copy(w_buf.at[1 - k], w_buf.at[1 - k], r_w.at[1 - k]).wait()
    for j in range(ROW):
        arrived(r_o, att, j)

    low = jnp.concatenate([att[0], att[1]], axis=1)
    high = jnp.concatenate([att[2], att[3]], axis=1)

    def toward(n):
        return (right, left) if n % 2 == 0 else (left, right)

    def project(cols):
        total = jnp.dot(low, w_buf[0, :, cols], preferred_element_type=jnp.float32)
        return total + jnp.dot(high, w_buf[1, :, cols], preferred_element_type=jnp.float32)

    def send(src, dst, s_sem, r_sem, target):
        return pltpu.make_async_remote_copy(
            src, dst, s_sem, r_sem, device_id=target, device_id_type=MESH
        )

    far = (x + 2) % NX

    def copy1(n):
        return send(part.at[n, far], got1.at[n], s1.at[n], r1.at[n], xdev(toward(n)[0]))

    def copy2(n):
        behind = toward(n)[1]
        return send(part.at[n, behind], got2.at[n], s2.at[n], r2.at[n], xdev(behind))

    def copy3(n):
        return send(send3.at[n], got3.at[n], s3.at[n], r3.at[n], xdev(toward(n)[0]))

    def copy4(n):
        return send(send4.at[n], got4.at[n], s4.at[n], r4.at[n], partner)

    def stage1(n):
        total = project(slice(n * CW, (n + 1) * CW))
        part[n] = total.astype(jnp.bfloat16).reshape(NX, 2 * OWN, CW)
        copy1(n).start()
        copy2(n).start()

    def stage2(n):
        copy1(n).wait_recv()
        own = part[n, toward(n)[0]].astype(jnp.float32)
        send3[n] = (own + got1[n].astype(jnp.float32)).astype(jnp.bfloat16)
        copy3(n).start()

    def stage3(n):
        copy2(n).wait_recv()
        copy3(n).wait_recv()
        total = part[n, x].astype(jnp.float32) + got2[n].astype(jnp.float32)
        total = total + got3[n].astype(jnp.float32)
        summed[n] = total.reshape(2, OWN, CW)
        send4[n] = summed[n, 1 - yh].astype(jnp.bfloat16)
        copy4(n).start()

    def stage4(n):
        copy4(n).wait_recv()
        total = summed[n, yh] + got4[n].astype(jnp.float32)
        out_ref[:, n * CW : (n + 1) * CW] = total.astype(jnp.bfloat16)

    def copy_y():
        return send(send_y, got_y, s_y, r_y, partner)

    def copy1_y(h):
        return send(
            half_y.at[h, far], got1_y.at[h], s1_y.at[h], r1_y.at[h], xdev(toward(h)[0])
        )

    def copy2_y(h):
        behind = toward(h)[1]
        return send(half_y.at[h, behind], got2_y.at[h], s2_y.at[h], r2_y.at[h], xdev(behind))

    def copy3_y(h):
        return send(send3_y.at[h], got3_y.at[h], s3_y.at[h], r3_y.at[h], xdev(toward(h)[0]))

    def first_y():
        part_y[...] = project(slice(XCOLS, D)).reshape(NX, 2, OWN, YW)
        send_y[...] = part_y[:, 1 - yh].astype(jnp.bfloat16)
        copy_y().start()

    def second_y():
        copy_y().wait_recv()
        total = part_y[:, yh] + got_y[...].astype(jnp.float32)
        for h in range(2):
            half_y[h] = total[:, :, h * YH : (h + 1) * YH].astype(jnp.bfloat16)
            copy1_y(h).start()
            copy2_y(h).start()

    def third_y():
        for h in range(2):
            copy1_y(h).wait_recv()
            total = half_y[h, toward(h)[0]].astype(jnp.float32) + got1_y[h].astype(jnp.float32)
            send3_y[h] = total.astype(jnp.bfloat16)
            copy3_y(h).start()

    def fourth_y():
        for h in range(2):
            copy2_y(h).wait_recv()
            copy3_y(h).wait_recv()
            total = half_y[h, x].astype(jnp.float32) + got2_y[h].astype(jnp.float32)
            total = total + got3_y[h].astype(jnp.float32)
            out_ref[:, XCOLS + h * YH : XCOLS + (h + 1) * YH] = total.astype(jnp.bfloat16)

    extra = {0: first_y, Y2: second_y, Y3: third_y, Y4: fourth_y}
    for step in range(CHUNKS + LAG4):
        for lag, stage in ((0, stage1), (LAG2, stage2), (LAG3, stage3), (LAG4, stage4)):
            if 0 <= step - lag < CHUNKS:
                stage(step - lag)
        if step in extra:
            extra[step]()

    for n in ORDER:
        for i in range(2):
            pl.when(2 * k + i != y)(lambda i=i, n=n: direct(i, n, True).wait_send())
    for a, n, b, target, there in plan:
        for j in range(2):
            if there is None:
                forward(n, b, a, target, j).wait_send()
            else:
                pl.when(there)(lambda: forward(n, b, a, target, j).wait_send())
    w_sib.wait_send()
    for i in range(2):
        for r in range(2):
            here = (2 * k + i == y) & (k == r)
            pl.when(jnp.logical_not(here))(lambda: home(i, r, True).wait_send())
    for n in range(CHUNKS):
        for copy in (copy1, copy2, copy3, copy4):
            copy(n).wait_send()
    copy_y().wait_send()
    for h in range(2):
        for copy in (copy1_y, copy2_y, copy3_y):
            copy(h).wait_send()


def local(queries, keys, values, out_weight, neighbours, counts):
    bf16, f32 = jnp.bfloat16, jnp.float32
    vmem, dma = pltpu.VMEM, pltpu.SemaphoreType.DMA
    window = vmem((8, TILE, HD), bf16)
    per_query = vmem((2, TILE, HD), f32)
    ring = vmem((CHUNKS, 2 * OWN, CW), bf16)
    owned = vmem((CHUNKS, OWN, CW), bf16)
    ring_y = vmem((2, OWN, YH), bf16)
    anywhere = pl.BlockSpec(memory_space=pltpu.HBM)
    operands = (queries, keys, values, out_weight, neighbours)
    return pl.pallas_call(
        body,
        out_shape=jax.ShapeDtypeStruct((OWN, D), bf16),
        in_specs=[anywhere] * 5 + [pl.BlockSpec(memory_space=pltpu.SMEM)],
        out_specs=pl.BlockSpec(memory_space=vmem),
        scratch_shapes=[
            pltpu.SMEM((1, 7), jnp.int32),
            vmem((2, TILE, HD), bf16), window, window,
            vmem((8, HD), f32), vmem((2, 8, HD), f32),
            vmem((2, TILE, 8 * TILE), f32), vmem((2, TILE, 8 * TILE), bf16),
            per_query, per_query, per_query,
            vmem((2, 2, HALF, HD), bf16), vmem((ROW, HALF, HD), bf16),
            vmem((2, 2 * HD, D), bf16),
            vmem((CHUNKS, NX, 2 * OWN, CW), bf16), ring, ring, ring, ring,
            vmem((CHUNKS, 2, OWN, CW), f32), owned, owned,
            vmem((NX, 2, OWN, YW), f32), vmem((NX, OWN, YW), bf16), vmem((NX, OWN, YW), bf16),
            vmem((2, NX, OWN, YH), bf16), ring_y, ring_y, ring_y, ring_y,
            dma((2, 4)), dma((2,)), dma((8,)), dma((8,)), dma((2,)), dma((2, 6)),
            dma((2, 2)), dma((ROW,)), dma, dma((2,)), dma,
        ] + [dma((CHUNKS,))] * 8 + [dma, dma] + [dma((2,))] * 6,
        compiler_params=pltpu.CompilerParams(
            collective_id=0, has_side_effects=True, vmem_limit_bytes=48 << 20
        ),
        name="tile_attention",
    )(*[pltpu.with_memory_space_constraint(a, pltpu.HBM) for a in operands], counts)


def solution(mesh):
    placed = (
        P("ctx", "head"),
        P("ctx", "head"),
        P("ctx", "head"),
        P("head", None),
        P("ctx", None),
        P("ctx"),
    )
    return jax.shard_map(
        local, mesh=mesh, in_specs=placed, out_specs=P(("ctx", "head"), None), check_vma=False
    )
```

time: 75.6 us -> 65.3 us (0.86)
  local copies, waits for them, and re-layouts: 5.86 us -> 0.7 us
  Pallas kernels: 68.8 us -> 63.8 us
    unnamed x11 -> x1, local copies, waits for them, and re-layouts: 5.86 us -> 0.7 us
    pallas_call x1, Pallas kernels: 68.8 us -> 63.8 us  [local(): pl.pallas_call(body, out_shape=jax.ShapeDtypeStruct((OWN, D), bf16), in_s...]
where the time goes in v2:
time: 65.3 us; the launch traced here: 65.2 us
  Pallas kernels  63.8 us (98%)
  local copies, waits for them, and re-layouts  0.7 us (1%)
  between operations  0.66 us (1%)
    pallas_call x1, Pallas kernels, local(): pl.pallas_call(body, out_shape=jax.ShapeDtypeStruct((OWN, D), bf16), in_s...  63.8 us

profile of v2, /device:TPU:8, one launch (start us, length us, event | category | flops | bytes accessed | tf_op | source)
XLA Modules:
  0.0 65.2 jit_solution(5018562007825189090)
XLA Ops:
  0.7 63.8 %tile_attention.1 = bf16[24,5120]{1,0:T(8,128)(2,1)S(1)} custom-call(bf16[384,256]{1,0:T(8,128)(2,1)} %q_hbm.1, bf16[384,256]{1,0:T(8,128)(2,1)} %k_hbm.1, bf16[384,256]{1,0:T(8,128)(2,1)} %v_hbm.1, bf16[256,5120]{1,0:T(8,128)(2,1)} %w_hbm.1, s32[1,7]{1,0:T(1,128)} %nb_hbm.1, s32[1]{0:T(128)S(6)} %copy.8.ct_ref), custom_call_target="tpu_custom_call" | custom-call | tf_op jit(solution)/shard_map/tile_attention/pallas_call | solution.py:446
  64.5 0.7 %copy.9 = bf16[24,5120]{1,0:T(8,128)(2,1)} copy(bf16[24,5120]{1,0:T(8,128)(2,1)S(1)} %tile_attention.1) | data formatting | bytes 491520

commit v3 on v2

--- a/solution.py
+++ b/solution.py
@@ -15,17 +15,13 @@
 NZ = 8
 NX = 4
 OWN = 24
-HALF = 192
+HALF = 96
 D = 5120
-CHUNKS = 9
-CW = 512
-YW = 512
-YH = YW // 2
-XCOLS = CHUNKS * CW
+CHUNKS = 8
+CW = D // CHUNKS
 MASKED = 1e30
 FACTOR = math.log2(math.e) / math.sqrt(HD)
-LAG2, LAG3, LAG4 = 2, 5, 9
-Y2, Y3, Y4 = CHUNKS + LAG2 - 1, CHUNKS + LAG3 - 1, CHUNKS + LAG4 - 2
+LAG2, LAG3 = 3, 6
 ORDER = (2, 1, 0, 3)
 
 
@@ -33,10 +29,9 @@
     q_hbm, k_hbm, v_hbm, w_hbm, nb_hbm, ct_ref, out_ref,
     nb_ref, q_win, k_win, v_win, bias_src, bias_win, score, weight, m_ref, l_ref, acc_ref,
     o_buf, att, w_buf,
-    part, got1, got2, got3, send3, summed, send4, got4,
-    part_y, send_y, got_y, half_y, got1_y, got2_y, got3_y, send3_y,
+    part, got1, got2, got3, send3, send4, got4,
     s_dir, r_q, r_k, r_v, r_b, s_fwd, s_o, r_o, s_w, r_w, s_nb,
-    s1, s2, s3, s4, r1, r2, r3, r4, s_y, r_y, s1_y, s2_y, s3_y, r1_y, r2_y, r3_y,
+    s1, s2, s3, r1, r2, r3, s4, r4,
 ):
     ctx = lax.axis_index("ctx")
     head = lax.axis_index("head")
@@ -276,42 +271,37 @@
 
     lax.fori_loop(0, 2, last_products, 0)
 
-    def home(i, r, remote):
-        src, dst = o_buf.at[i, r], att.at[y]
+    def side(p):
+        return (1 - yh) + p * (2 * yh - 1)
+
+    def home(p, i, r, remote):
+        src, dst = o_buf.at[i, r, side(p)], att.at[p, y]
         if remote:
             return pltpu.make_async_remote_copy(
-                src, dst, s_o.at[i, r], r_o.at[y],
+                src, dst, s_o.at[p, i, r], r_o.at[p, y],
                 device_id=dev(z, 2 * k + i, r), device_id_type=MESH,
             )
-        return pltpu.make_async_copy(src, dst, r_o.at[y])
+        return pltpu.make_async_copy(src, dst, r_o.at[p, y])
 
     for i in range(2):
         mixed = acc_ref[i] * (1.0 / jnp.sum(l_ref[i], axis=1, keepdims=True))
         for r in range(2):
-            pieces = [
-                mixed[OWN * (8 * h + 2 * xx + r) : OWN * (8 * h + 2 * xx + r + 1)]
-                for xx in range(NX)
-                for h in range(2)
-            ]
-            o_buf[i, r] = jnp.concatenate(pieces, axis=0).astype(jnp.bfloat16)
-            here = (2 * k + i == y) & (k == r)
-            pl.when(jnp.logical_not(here))(lambda: home(i, r, True).start())
-            pl.when(here)(lambda: home(i, r, False).start())
+            for h in range(2):
+                first_rows = [OWN * (8 * h + 2 * xx + r) for xx in range(NX)]
+                pieces = [mixed[at : at + OWN] for at in first_rows]
+                o_buf[i, r, h] = jnp.concatenate(pieces, axis=0).astype(jnp.bfloat16)
+    for p in range(2):
+        for i in range(2):
+            for r in range(2):
+                here = (2 * k + i == y) & (k == r)
+                pl.when(jnp.logical_not(here))(lambda: home(p, i, r, True).start())
+                pl.when(here)(lambda: home(p, i, r, False).start())
 
     w_own.wait()
     pltpu.make_async_copy(w_buf.at[1 - k], w_buf.at[1 - k], r_w.at[1 - k]).wait()
-    for j in range(ROW):
-        arrived(r_o, att, j)
-
-    low = jnp.concatenate([att[0], att[1]], axis=1)
-    high = jnp.concatenate([att[2], att[3]], axis=1)
-
-    def toward(n):
-        return (right, left) if n % 2 == 0 else (left, right)
-
-    def project(cols):
-        total = jnp.dot(low, w_buf[0, :, cols], preferred_element_type=jnp.float32)
-        return total + jnp.dot(high, w_buf[1, :, cols], preferred_element_type=jnp.float32)
+
+    def toward(c):
+        return (right, left) if c % 2 == 0 else (left, right)
 
     def send(src, dst, s_sem, r_sem, target):
         return pltpu.make_async_remote_copy(
@@ -320,95 +310,61 @@
 
     far = (x + 2) % NX
 
-    def copy1(n):
-        return send(part.at[n, far], got1.at[n], s1.at[n], r1.at[n], xdev(toward(n)[0]))
-
-    def copy2(n):
-        behind = toward(n)[1]
-        return send(part.at[n, behind], got2.at[n], s2.at[n], r2.at[n], xdev(behind))
-
-    def copy3(n):
-        return send(send3.at[n], got3.at[n], s3.at[n], r3.at[n], xdev(toward(n)[0]))
+    def copy1(c):
+        return send(part.at[c, far], got1.at[c], s1.at[c], r1.at[c], xdev(toward(c)[0]))
+
+    def copy2(c):
+        behind = toward(c)[1]
+        return send(part.at[c, behind], got2.at[c], s2.at[c], r2.at[c], xdev(behind))
+
+    def copy3(c):
+        return send(send3.at[c], got3.at[c], s3.at[c], r3.at[c], xdev(toward(c)[0]))
 
     def copy4(n):
         return send(send4.at[n], got4.at[n], s4.at[n], r4.at[n], partner)
 
-    def stage1(n):
-        total = project(slice(n * CW, (n + 1) * CW))
-        part[n] = total.astype(jnp.bfloat16).reshape(NX, 2 * OWN, CW)
-        copy1(n).start()
-        copy2(n).start()
-
-    def stage2(n):
-        copy1(n).wait_recv()
-        own = part[n, toward(n)[0]].astype(jnp.float32)
-        send3[n] = (own + got1[n].astype(jnp.float32)).astype(jnp.bfloat16)
-        copy3(n).start()
-
-    def stage3(n):
-        copy2(n).wait_recv()
-        copy3(n).wait_recv()
-        total = part[n, x].astype(jnp.float32) + got2[n].astype(jnp.float32)
-        total = total + got3[n].astype(jnp.float32)
-        summed[n] = total.reshape(2, OWN, CW)
-        send4[n] = summed[n, 1 - yh].astype(jnp.bfloat16)
-        copy4(n).start()
-
-    def stage4(n):
-        copy4(n).wait_recv()
-        total = summed[n, yh] + got4[n].astype(jnp.float32)
-        out_ref[:, n * CW : (n + 1) * CW] = total.astype(jnp.bfloat16)
-
-    def copy_y():
-        return send(send_y, got_y, s_y, r_y, partner)
-
-    def copy1_y(h):
-        return send(
-            half_y.at[h, far], got1_y.at[h], s1_y.at[h], r1_y.at[h], xdev(toward(h)[0])
-        )
-
-    def copy2_y(h):
-        behind = toward(h)[1]
-        return send(half_y.at[h, behind], got2_y.at[h], s2_y.at[h], r2_y.at[h], xdev(behind))
-
-    def copy3_y(h):
-        return send(send3_y.at[h], got3_y.at[h], s3_y.at[h], r3_y.at[h], xdev(toward(h)[0]))
-
-    def first_y():
-        part_y[...] = project(slice(XCOLS, D)).reshape(NX, 2, OWN, YW)
-        send_y[...] = part_y[:, 1 - yh].astype(jnp.bfloat16)
-        copy_y().start()
-
-    def second_y():
-        copy_y().wait_recv()
-        total = part_y[:, yh] + got_y[...].astype(jnp.float32)
-        for h in range(2):
-            half_y[h] = total[:, :, h * YH : (h + 1) * YH].astype(jnp.bfloat16)
-            copy1_y(h).start()
-            copy2_y(h).start()
-
-    def third_y():
-        for h in range(2):
-            copy1_y(h).wait_recv()
-            total = half_y[h, toward(h)[0]].astype(jnp.float32) + got1_y[h].astype(jnp.float32)
-            send3_y[h] = total.astype(jnp.bfloat16)
-            copy3_y(h).start()
-
-    def fourth_y():
-        for h in range(2):
-            copy2_y(h).wait_recv()
-            copy3_y(h).wait_recv()
-            total = half_y[h, x].astype(jnp.float32) + got2_y[h].astype(jnp.float32)
-            total = total + got3_y[h].astype(jnp.float32)
-            out_ref[:, XCOLS + h * YH : XCOLS + (h + 1) * YH] = total.astype(jnp.bfloat16)
-
-    extra = {0: first_y, Y2: second_y, Y3: third_y, Y4: fourth_y}
-    for step in range(CHUNKS + LAG4):
-        for lag, stage in ((0, stage1), (LAG2, stage2), (LAG3, stage3), (LAG4, stage4)):
-            if 0 <= step - lag < CHUNKS:
+    inputs = []
+
+    def stage1(c):
+        p, n = c // CHUNKS, c % CHUNKS
+        if n == 0:
+            for j in range(ROW):
+                pltpu.make_async_copy(att.at[p, j], att.at[p, j], r_o.at[p, j]).wait()
+            inputs.append(
+                [jnp.concatenate([att[p, j], att[p, j + 1]], axis=1) for j in (0, 2)]
+            )
+        low, high = inputs[p]
+        cols = slice(n * CW, (n + 1) * CW)
+        total = jnp.dot(low, w_buf[0, :, cols], preferred_element_type=jnp.float32)
+        total = total + jnp.dot(high, w_buf[1, :, cols], preferred_element_type=jnp.float32)
+        part[c] = total.reshape(NX, OWN, CW).astype(jnp.bfloat16)
+        copy1(c).start()
+        copy2(c).start()
+
+    def stage2(c):
+        copy1(c).wait_recv()
+        own = part[c, toward(c)[0]].astype(jnp.float32)
+        send3[c] = (own + got1[c].astype(jnp.float32)).astype(jnp.bfloat16)
+        copy3(c).start()
+
+    def stage3(c):
+        p, n = c // CHUNKS, c % CHUNKS
+        copy2(c).wait_recv()
+        copy3(c).wait_recv()
+        total = part[c, x].astype(jnp.float32) + got2[c].astype(jnp.float32)
+        total = total + got3[c].astype(jnp.float32)
+        if p == 0:
+            send4[n] = total.astype(jnp.bfloat16)
+            copy4(n).start()
+        else:
+            copy4(n).wait_recv()
+            total = total + got4[n].astype(jnp.float32)
+            out_ref[:, n * CW : (n + 1) * CW] = total.astype(jnp.bfloat16)
+
+    for step in range(2 * CHUNKS + LAG3):
+        for lag, stage in ((0, stage1), (LAG2, stage2), (LAG3, stage3)):
+            if 0 <= step - lag < 2 * CHUNKS:
                 stage(step - lag)
-        if step in extra:
-            extra[step]()
 
     for n in ORDER:
         for i in range(2):
@@ -420,17 +376,16 @@
             else:
                 pl.when(there)(lambda: forward(n, b, a, target, j).wait_send())
     w_sib.wait_send()
-    for i in range(2):
-        for r in range(2):
-            here = (2 * k + i == y) & (k == r)
-            pl.when(jnp.logical_not(here))(lambda: home(i, r, True).wait_send())
+    for p in range(2):
+        for i in range(2):
+            for r in range(2):
+                here = (2 * k + i == y) & (k == r)
+                pl.when(jnp.logical_not(here))(lambda: home(p, i, r, True).wait_send())
+    for c in range(2 * CHUNKS):
+        for copy in (copy1, copy2, copy3):
+            copy(c).wait_send()
     for n in range(CHUNKS):
-        for copy in (copy1, copy2, copy3, copy4):
-            copy(n).wait_send()
-    copy_y().wait_send()
-    for h in range(2):
-        for copy in (copy1_y, copy2_y, copy3_y):
-            copy(h).wait_send()
+        copy4(n).wait_send()
 
 
 def local(queries, keys, values, out_weight, neighbours, counts):
@@ -438,9 +393,8 @@
     vmem, dma = pltpu.VMEM, pltpu.SemaphoreType.DMA
     window = vmem((8, TILE, HD), bf16)
     per_query = vmem((2, TILE, HD), f32)
-    ring = vmem((CHUNKS, 2 * OWN, CW), bf16)
+    ring = vmem((2 * CHUNKS, OWN, CW), bf16)
     owned = vmem((CHUNKS, OWN, CW), bf16)
-    ring_y = vmem((2, OWN, YH), bf16)
     anywhere = pl.BlockSpec(memory_space=pltpu.HBM)
     operands = (queries, keys, values, out_weight, neighbours)
     return pl.pallas_call(
@@ -454,15 +408,12 @@
             vmem((8, HD), f32), vmem((2, 8, HD), f32),
             vmem((2, TILE, 8 * TILE), f32), vmem((2, TILE, 8 * TILE), bf16),
             per_query, per_query, per_query,
-            vmem((2, 2, HALF, HD), bf16), vmem((ROW, HALF, HD), bf16),
+            vmem((2, 2, 2, HALF, HD), bf16), vmem((2, ROW, HALF, HD), bf16),
             vmem((2, 2 * HD, D), bf16),
-            vmem((CHUNKS, NX, 2 * OWN, CW), bf16), ring, ring, ring, ring,
-            vmem((CHUNKS, 2, OWN, CW), f32), owned, owned,
-            vmem((NX, 2, OWN, YW), f32), vmem((NX, OWN, YW), bf16), vmem((NX, OWN, YW), bf16),
-            vmem((2, NX, OWN, YH), bf16), ring_y, ring_y, ring_y, ring_y,
+            vmem((2 * CHUNKS, NX, OWN, CW), bf16), ring, ring, ring, ring, owned, owned,
             dma((2, 4)), dma((2,)), dma((8,)), dma((8,)), dma((2,)), dma((2, 6)),
-            dma((2, 2)), dma((ROW,)), dma, dma((2,)), dma,
-        ] + [dma((CHUNKS,))] * 8 + [dma, dma] + [dma((2,))] * 6,
+            dma((2, 2, 2)), dma((2, ROW)), dma, dma((2,)), dma,
+        ] + [dma((2 * CHUNKS,))] * 6 + [dma((CHUNKS,))] * 2,
         compiler_params=pltpu.CompilerParams(
             collective_id=0, has_side_effects=True, vmem_limit_bytes=48 << 20
         ),

time: 65.3 us -> 61.1 us (0.936)
  the two profiles are of different devices: /device:TPU:8 before, /device:TPU:60 now
where the time goes in v3:
time: 61.1 us; the launch traced here: 60.9 us
  Pallas kernels  59.6 us (98%)
  local copies, waits for them, and re-layouts  0.7 us (1%)
  between operations  0.66 us (1%)
    pallas_call x1, Pallas kernels, local(): pl.pallas_call(body, out_shape=jax.ShapeDtypeStruct((OWN, D), bf16), in_s...  59.6 us

profile of v3, /device:TPU:60, one launch (start us, length us, event | category | flops | bytes accessed | tf_op | source)
XLA Modules:
  0.0 60.9 jit_solution(15236114993810467773)
XLA Ops:
  0.7 59.6 %tile_attention.1 = bf16[24,5120]{1,0:T(8,128)(2,1)S(1)} custom-call(bf16[384,256]{1,0:T(8,128)(2,1)} %q_hbm.1, bf16[384,256]{1,0:T(8,128)(2,1)} %k_hbm.1, bf16[384,256]{1,0:T(8,128)(2,1)} %v_hbm.1, bf16[256,5120]{1,0:T(8,128)(2,1)} %w_hbm.1, s32[1,7]{1,0:T(1,128)} %nb_hbm.1, s32[1]{0:T(128)S(6)} %copy.8.ct_ref), custom_call_target="tpu_custom_call" | custom-call | tf_op jit(solution)/shard_map/tile_attention/pallas_call | solution.py:400
  60.2 0.7 %copy.9 = bf16[24,5120]{1,0:T(8,128)(2,1)} copy(bf16[24,5120]{1,0:T(8,128)(2,1)S(1)} %tile_attention.1) | data formatting | bytes 491520

commit v4 on v3

--- a/solution.py
+++ b/solution.py
@@ -17,8 +17,7 @@
 OWN = 24
 HALF = 96
 D = 5120
-CHUNKS = 8
-CW = D // CHUNKS
+WIDTHS = (640,) * 8
 MASKED = 1e30
 FACTOR = math.log2(math.e) / math.sqrt(HD)
 LAG2, LAG3 = 3, 6
@@ -31,7 +30,7 @@
     o_buf, att, w_buf,
     part, got1, got2, got3, send3, send4, got4,
     s_dir, r_q, r_k, r_v, r_b, s_fwd, s_o, r_o, s_w, r_w, s_nb,
-    s1, s2, s3, r1, r2, r3, s4, r4,
+    s1, s2, s3, s4, r1, r2, r3, r4,
 ):
     ctx = lax.axis_index("ctx")
     head = lax.axis_index("head")
@@ -112,15 +111,16 @@
             )
         return pltpu.make_async_copy(src, dst, sem)
 
+    w_sib = pltpu.make_async_remote_copy(
+        w_hbm, w_buf.at[k], s_w, r_w.at[k], device_id=sibling, device_id_type=MESH
+    )
+
     for n in ORDER:
+        if n == 0:
+            w_sib.start()
         for i in range(2):
             pl.when(2 * k + i != y)(lambda i=i, n=n: direct(i, n, True).start())
             pl.when(2 * k + i == y)(lambda i=i, n=n: direct(i, n, False).start())
-
-    w_sib = pltpu.make_async_remote_copy(
-        w_hbm, w_buf.at[k], s_w, r_w.at[k], device_id=sibling, device_id_type=MESH
-    )
-    w_sib.start()
 
     windows = ((k_win, r_k), (v_win, r_v))
     plan = (
@@ -224,6 +224,7 @@
     lax.fori_loop(0, 2, last_scores, 0)
 
     take(3, 1)
+    take(4, 1)
     for i in range(2):
         m_ref[i] = jnp.broadcast_to(jnp.max(m_ref[i], axis=1, keepdims=True), (TILE, HD))
 
@@ -233,7 +234,6 @@
         return carry
 
     lax.fori_loop(0, 3, weigh_both, 0)
-    take(4, 1)
     lax.fori_loop(3, 7, weigh_both, 0)
 
     arrived(r_v, v_win, slot(5))
@@ -297,75 +297,6 @@
                 pl.when(jnp.logical_not(here))(lambda: home(p, i, r, True).start())
                 pl.when(here)(lambda: home(p, i, r, False).start())
 
-    w_own.wait()
-    pltpu.make_async_copy(w_buf.at[1 - k], w_buf.at[1 - k], r_w.at[1 - k]).wait()
-
-    def toward(c):
-        return (right, left) if c % 2 == 0 else (left, right)
-
-    def send(src, dst, s_sem, r_sem, target):
-        return pltpu.make_async_remote_copy(
-            src, dst, s_sem, r_sem, device_id=target, device_id_type=MESH
-        )
-
-    far = (x + 2) % NX
-
-    def copy1(c):
-        return send(part.at[c, far], got1.at[c], s1.at[c], r1.at[c], xdev(toward(c)[0]))
-
-    def copy2(c):
-        behind = toward(c)[1]
-        return send(part.at[c, behind], got2.at[c], s2.at[c], r2.at[c], xdev(behind))
-
-    def copy3(c):
-        return send(send3.at[c], got3.at[c], s3.at[c], r3.at[c], xdev(toward(c)[0]))
-
-    def copy4(n):
-        return send(send4.at[n], got4.at[n], s4.at[n], r4.at[n], partner)
-
-    inputs = []
-
-    def stage1(c):
-        p, n = c // CHUNKS, c % CHUNKS
-        if n == 0:
-            for j in range(ROW):
-                pltpu.make_async_copy(att.at[p, j], att.at[p, j], r_o.at[p, j]).wait()
-            inputs.append(
-                [jnp.concatenate([att[p, j], att[p, j + 1]], axis=1) for j in (0, 2)]
-            )
-        low, high = inputs[p]
-        cols = slice(n * CW, (n + 1) * CW)
-        total = jnp.dot(low, w_buf[0, :, cols], preferred_element_type=jnp.float32)
-        total = total + jnp.dot(high, w_buf[1, :, cols], preferred_element_type=jnp.float32)
-        part[c] = total.reshape(NX, OWN, CW).astype(jnp.bfloat16)
-        copy1(c).start()
-        copy2(c).start()
-
-    def stage2(c):
-        copy1(c).wait_recv()
-        own = part[c, toward(c)[0]].astype(jnp.float32)
-        send3[c] = (own + got1[c].astype(jnp.float32)).astype(jnp.bfloat16)
-        copy3(c).start()
-
-    def stage3(c):
-        p, n = c // CHUNKS, c % CHUNKS
-        copy2(c).wait_recv()
-        copy3(c).wait_recv()
-        total = part[c, x].astype(jnp.float32) + got2[c].astype(jnp.float32)
-        total = total + got3[c].astype(jnp.float32)
-        if p == 0:
-            send4[n] = total.astype(jnp.bfloat16)
-            copy4(n).start()
-        else:
-            copy4(n).wait_recv()
-            total = total + got4[n].astype(jnp.float32)
-            out_ref[:, n * CW : (n + 1) * CW] = total.astype(jnp.bfloat16)
-
-    for step in range(2 * CHUNKS + LAG3):
-        for lag, stage in ((0, stage1), (LAG2, stage2), (LAG3, stage3)):
-            if 0 <= step - lag < 2 * CHUNKS:
-                stage(step - lag)
-
     for n in ORDER:
         for i in range(2):
             pl.when(2 * k + i != y)(lambda i=i, n=n: direct(i, n, True).wait_send())
@@ -376,16 +307,100 @@
             else:
                 pl.when(there)(lambda: forward(n, b, a, target, j).wait_send())
     w_sib.wait_send()
+    w_own.wait()
+    pltpu.make_async_copy(w_buf.at[1 - k], w_buf.at[1 - k], r_w.at[1 - k]).wait()
+
+    chunks = []
+    for p in range(2):
+        start = 0
+        for width in WIDTHS:
+            chunks.append((p, slice(start, start + width)))
+            start += width
+
+    def toward(c):
+        ahead = (x + 1 + 2 * ((c + k) % 2)) % NX
+        return ahead, (ahead + 2) % NX
+
+    def send(src, dst, s_sem, r_sem, target):
+        return pltpu.make_async_remote_copy(
+            src, dst, s_sem, r_sem, device_id=target, device_id_type=MESH
+        )
+
+    far = (x + 2) % NX
+
+    def copy1(c):
+        p, cols = chunks[c]
+        return send(
+            part.at[p, far, :, cols], got1.at[p, :, cols], s1, r1.at[c], xdev(toward(c)[0])
+        )
+
+    def copy2(c):
+        p, cols = chunks[c]
+        behind = toward(c)[1]
+        return send(
+            part.at[p, behind, :, cols], got2.at[p, :, cols], s2, r2.at[c], xdev(behind)
+        )
+
+    def copy3(c):
+        p, cols = chunks[c]
+        return send(
+            send3.at[p, :, cols], got3.at[p, :, cols], s3, r3.at[c], xdev(toward(c)[0])
+        )
+
+    def copy4(cols, n):
+        return send(send4.at[:, cols], got4.at[:, cols], s4, r4.at[n], partner)
+
+    inputs = []
+
+    def stage1(c):
+        p, cols = chunks[c]
+        if cols.start == 0:
+            for j in range(ROW):
+                pltpu.make_async_copy(att.at[p, j], att.at[p, j], r_o.at[p, j]).wait()
+            inputs.append(
+                [jnp.concatenate([att[p, j], att[p, j + 1]], axis=1) for j in (0, 2)]
+            )
+        low, high = inputs[p]
+        total = jnp.dot(low, w_buf[0, :, cols], preferred_element_type=jnp.float32)
+        total = total + jnp.dot(high, w_buf[1, :, cols], preferred_element_type=jnp.float32)
+        width = cols.stop - cols.start
+        part[p, :, :, cols] = total.reshape(NX, OWN, width).astype(jnp.bfloat16)
+        copy1(c).start()
+        copy2(c).start()
+
+    def stage2(c):
+        p, cols = chunks[c]
+        copy1(c).wait_recv()
+        own = part[p, toward(c)[0], :, cols].astype(jnp.float32)
+        send3[p, :, cols] = (own + got1[p, :, cols].astype(jnp.float32)).astype(jnp.bfloat16)
+        copy3(c).start()
+
+    def stage3(c):
+        p, cols = chunks[c]
+        copy2(c).wait_recv()
+        copy3(c).wait_recv()
+        total = part[p, x, :, cols].astype(jnp.float32) + got2[p, :, cols].astype(jnp.float32)
+        total = total + got3[p, :, cols].astype(jnp.float32)
+        if p == 0:
+            send4[:, cols] = total.astype(jnp.bfloat16)
+            copy4(cols, c).start()
+        else:
+            copy4(cols, c - len(WIDTHS)).wait_recv()
+            total = total + got4[:, cols].astype(jnp.float32)
+            out_ref[:, cols] = total.astype(jnp.bfloat16)
+
+    for step in range(len(chunks) + LAG3):
+        for lag, stage in ((0, stage1), (LAG2, stage2), (LAG3, stage3)):
+            if 0 <= step - lag < len(chunks):
+                stage(step - lag)
+
     for p in range(2):
         for i in range(2):
             for r in range(2):
                 here = (2 * k + i == y) & (k == r)
                 pl.when(jnp.logical_not(here))(lambda: home(p, i, r, True).wait_send())
-    for c in range(2 * CHUNKS):
-        for copy in (copy1, copy2, copy3):
-            copy(c).wait_send()
-    for n in range(CHUNKS):
-        copy4(n).wait_send()
+    for landed, sem in ((got1, s1), (got2, s2), (got3, s3), (got4, s4)):
+        pltpu.make_async_copy(landed, landed, sem).wait()
 
 
 def local(queries, keys, values, out_weight, neighbours, counts):
@@ -393,8 +408,9 @@
     vmem, dma = pltpu.VMEM, pltpu.SemaphoreType.DMA
     window = vmem((8, TILE, HD), bf16)
     per_query = vmem((2, TILE, HD), f32)
-    ring = vmem((2 * CHUNKS, OWN, CW), bf16)
-    owned = vmem((CHUNKS, OWN, CW), bf16)
+    ring = vmem((2, OWN, D), bf16)
+    owned = vmem((OWN, D), bf16)
+    chunks = 2 * len(WIDTHS)
     anywhere = pl.BlockSpec(memory_space=pltpu.HBM)
     operands = (queries, keys, values, out_weight, neighbours)
     return pl.pallas_call(
@@ -410,10 +426,10 @@
             per_query, per_query, per_query,
             vmem((2, 2, 2, HALF, HD), bf16), vmem((2, ROW, HALF, HD), bf16),
             vmem((2, 2 * HD, D), bf16),
-            vmem((2 * CHUNKS, NX, OWN, CW), bf16), ring, ring, ring, ring, owned, owned,
+            vmem((2, NX, OWN, D), bf16), ring, ring, ring, ring, owned, owned,
             dma((2, 4)), dma((2,)), dma((8,)), dma((8,)), dma((2,)), dma((2, 6)),
             dma((2, 2, 2)), dma((2, ROW)), dma, dma((2,)), dma,
-        ] + [dma((2 * CHUNKS,))] * 6 + [dma((CHUNKS,))] * 2,
+        ] + [dma] * 4 + [dma((chunks,))] * 4,
         compiler_params=pltpu.CompilerParams(
             collective_id=0, has_side_effects=True, vmem_limit_bytes=48 << 20
         ),

time: 61.1 us -> 60.4 us (0.989)
  Pallas kernels: 59.6 us -> 58.9 us
    pallas_call x1, Pallas kernels: 59.6 us -> 58.9 us  [local(): pl.pallas_call(body, out_shape=jax.ShapeDtypeStruct((OWN, D), bf16), in_s...]
where the time goes in v4:
time: 60.4 us; the launch traced here: 60.2 us
  Pallas kernels  58.9 us (98%)
  local copies, waits for them, and re-layouts  0.7 us (1%)
  between operations  0.66 us (1%)
    pallas_call x1, Pallas kernels, local(): pl.pallas_call(body, out_shape=jax.ShapeDtypeStruct((OWN, D), bf16), in_s...  58.9 us

profile of v4, /device:TPU:60, one launch (start us, length us, event | category | flops | bytes accessed | tf_op | source)
XLA Modules:
  0.0 60.2 jit_solution(17065494976689120993)
XLA Ops:
  0.7 58.9 %tile_attention.1 = bf16[24,5120]{1,0:T(8,128)(2,1)S(1)} custom-call(bf16[384,256]{1,0:T(8,128)(2,1)} %q_hbm.1, bf16[384,256]{1,0:T(8,128)(2,1)} %k_hbm.1, bf16[384,256]{1,0:T(8,128)(2,1)} %v_hbm.1, bf16[256,5120]{1,0:T(8,128)(2,1)} %w_hbm.1, s32[1,7]{1,0:T(1,128)} %nb_hbm.1, s32[1]{0:T(128)S(6)} %copy.8.ct_ref), custom_call_target="tpu_custom_call" | custom-call | tf_op jit(solution)/shard_map/tile_attention/pallas_call | solution.py:416
  59.5 0.7 %copy.9 = bf16[24,5120]{1,0:T(8,128)(2,1)} copy(bf16[24,5120]{1,0:T(8,128)(2,1)S(1)} %tile_attention.1) | data formatting | bytes 491520
